TPU v7x, 32 devices: a whole 2x2x4 slice. The times are simulated.
32 devices in a mesh: row: 4 (over z), col: 8 (over y, x, core).
Axes of the slice: x: 2, y: 2, z: 4, core: 2. Of those that a mesh axis runs over, the one named last changes fastest.
Arguments:
- tokens: bfloat16 [2, 96, 128, 512], P(None, 'row', 'col'), may hold values from -6 to 6
- w_qkv: bfloat16 [512, 1536], replicated, may hold values from -0.25 to 0.25
- w_out: bfloat16 [512, 512], replicated, may hold values from -0.25 to 0.25
- q_saved: bfloat16 [2, 96, 128, 512], P(None, 'row', 'col'), may hold values from -4 to 4
- k_saved: bfloat16 [2, 96, 128, 512], P(None, 'row', 'col'), may hold values from -4 to 4
- v_saved: bfloat16 [2, 96, 128, 512], P(None, 'row', 'col'), may hold values from -4 to 4
- scale_exp: int32 [2, 12, 16, 24], P(None, 'row', 'col'), may hold values from -1 to 1
- grad_out: bfloat16 [2, 96, 128, 512], P(None, 'row', 'col'), may hold values from -6 to 6
- crop_start: int32 [2, 2], replicated, may hold values from 0 to 3
Outputs:
- grad_tokens: bfloat16 [2, 96, 128, 512], P(None, 'row', 'col')
- grad_w_qkv: float32 [512, 1536], P('row', 'col')
- grad_w_out: float32 [512, 512], P('row', 'col')
Inputs may be any that keep to these rules, and one draw needn't show every extreme that they name: crop_start[b] holds the first row and the first column of the region of frame b that the loss covers.
All inputs are finite; a program needn't handle non-finite values.
Results may differ from a plain program's by a relative error of at most 0.017.
Values may be sent and summed in bfloat16 or wider, within the bound.
A program may use at most 128 MiB of HBM per device.

v0:
```python
import math
import jax
import jax.numpy as jnp
from jax import lax
from jax.sharding import PartitionSpec as P

HEADS = 8
RADIUS = 4
BLOCK = 8
max_norm = 1000.0
masked_score = -1e30
tiny_square = 1e-06


def passed_along(array, axis, by):
    size = lax.axis_size(axis)
    pairs = [(i, i + by) for i in range(size) if 0 <= i + by < size]
    return lax.ppermute(array, axis, pairs)


def padded_2(cells, sides, width):
    for axis, dim in sides:
        count = lax.axis_size(axis)
        ends = count - 1
        head = lax.slice_in_dim(cells, 0, width, axis=dim)
        tail = lax.slice_in_dim(cells, cells.shape[dim] - width, cells.shape[dim], axis=dim)
        cells = jnp.concatenate(
            [
                lax.ppermute(tail, axis, [(i, (i + 1) % count) for i in range(ends)]),
                cells,
                lax.ppermute(head, axis, [((i + 1) % count, i) for i in range(ends)]),
            ],
            axis=dim,
        )
    return cells


def product(form, left, right):
    return jnp.einsum(form, left, right, preferred_element_type=jnp.float32)


def dequantize(mantissa, exponent):
    members, height, breadth, features = mantissa.shape
    heads = exponent.shape[3]
    factor = jnp.exp2(exponent.astype(jnp.float32))
    factor = jnp.repeat(jnp.repeat(factor, BLOCK, axis=1), BLOCK, axis=2)
    scaled = (
        mantissa.astype(jnp.float32).reshape(members, height, breadth, heads, features // heads)
        * factor[..., None]
    )
    return scaled.reshape(members, height, breadth, features).astype(jnp.bfloat16)


def query_tiles(tensor):
    height, breadth, features = tensor.shape
    blocked = tensor.reshape(
        height // BLOCK, BLOCK, breadth // BLOCK, BLOCK, HEADS, features // HEADS
    )
    return blocked.transpose(0, 2, 1, 3, 4, 5).reshape(
        height // BLOCK, breadth // BLOCK, BLOCK * BLOCK, HEADS, features // HEADS
    )


def query_untile(tile_set, height, breadth):
    tile_rows, tile_cols = (tile_set.shape[0], tile_set.shape[1])
    features = tile_set.shape[3] * tile_set.shape[4]
    blocked = tile_set.reshape(tile_rows, tile_cols, BLOCK, BLOCK, features)
    return blocked.transpose(0, 2, 1, 3, 4).reshape(height, breadth, features)


def key_tiles(padded):
    height, breadth, features = padded.shape
    tile_rows = height // BLOCK - 1
    tile_cols = breadth // BLOCK - 1
    blocked = padded.reshape(tile_rows + 1, BLOCK, tile_cols + 1, BLOCK, features)
    paired = jnp.stack([blocked[:-1], blocked[1:]], axis=1).reshape(
        tile_rows, 2 * BLOCK, tile_cols + 1, BLOCK, features
    )
    paired = jnp.stack([paired[:, :, :-1], paired[:, :, 1:]], axis=3).reshape(
        tile_rows, 2 * BLOCK, tile_cols, 2 * BLOCK, features
    )
    return paired.transpose(0, 2, 1, 3, 4).reshape(
        tile_rows, tile_cols, 4 * BLOCK * BLOCK, HEADS, features // HEADS
    )


def fold_keys(tile_set):
    tile_rows, tile_cols = (tile_set.shape[0], tile_set.shape[1])
    features = tile_set.shape[3] * tile_set.shape[4]
    tile_grid = tile_set.reshape(tile_rows, tile_cols, 2, BLOCK, 2, BLOCK, features).transpose(
        0, 2, 3, 1, 4, 5, 6
    )
    zero_row = jnp.zeros((1, BLOCK, tile_cols, 2, BLOCK, features), tile_set.dtype)
    summed = jnp.concatenate([tile_grid[:, 0], zero_row], 0) + jnp.concatenate(
        [zero_row, tile_grid[:, 1]], 0
    )
    zero_col = jnp.zeros((tile_rows + 1, BLOCK, 1, BLOCK, features), tile_set.dtype)
    summed = jnp.concatenate([summed[:, :, :, 0], zero_col], 2) + jnp.concatenate(
        [zero_col, summed[:, :, :, 1]], 2
    )
    return summed.reshape((tile_rows + 1) * BLOCK, (tile_cols + 1) * BLOCK, features)


def key_valid(anchor, tile_count, extent):
    position = (
        anchor
        + BLOCK * jnp.arange(tile_count, dtype=jnp.int32)[:, None]
        + jnp.arange(2 * BLOCK, dtype=jnp.int32)[None, :]
    )
    return (position >= 0) & (position < extent)


def window_mask():
    reach = (
        jnp.arange(2 * BLOCK, dtype=jnp.int32)[None, :]
        - jnp.arange(BLOCK, dtype=jnp.int32)[:, None]
    )
    inside = (reach >= 0) & (reach <= 2 * RADIUS)
    return (inside[:, None, :, None] & inside[None, :, None, :]).reshape(
        BLOCK * BLOCK, 4 * BLOCK * BLOCK
    )


def attend(
    queries, grads_attn, keys_pad, values_pad, row_anchor, col_anchor, frame_rows, frame_cols
):
    height, breadth, features = queries.shape
    score_scale = 1.0 / math.sqrt(features // HEADS)
    q_tiles = query_tiles(queries)
    g_tiles = query_tiles(grads_attn)
    k_tiles = key_tiles(keys_pad)
    v_tiles = key_tiles(values_pad)
    tile_rows, tile_cols = (q_tiles.shape[0], q_tiles.shape[1])
    row_ok = key_valid(row_anchor, tile_rows, frame_rows)
    col_ok = key_valid(col_anchor, tile_cols, frame_cols)
    keys_ok = (row_ok[:, None, :, None] & col_ok[None, :, None, :]).reshape(
        tile_rows, tile_cols, 1, 1, 4 * BLOCK * BLOCK
    )
    allowed = keys_ok & window_mask()[None, None, None]
    scores = product("ijqhd,ijkhd->ijhqk", q_tiles, k_tiles) * score_scale
    scores = jnp.where(allowed, scores, masked_score)
    row_max = jnp.max(scores, axis=-1, keepdims=True)
    weights = jnp.exp(scores - row_max)
    softmax = weights / jnp.sum(weights, axis=-1, keepdims=True)
    softmax_half = softmax.astype(jnp.bfloat16)
    out_tiles = product("ijhqk,ijkhd->ijqhd", softmax_half, v_tiles).astype(jnp.bfloat16)
    row_delta = product("ijqhd,ijqhd->ijhq", g_tiles, out_tiles)
    grad_probs = product("ijqhd,ijkhd->ijhqk", g_tiles, v_tiles)
    grad_scores = (softmax * (grad_probs - row_delta[..., None]) * score_scale).astype(jnp.bfloat16)
    grad_q_tiles = product("ijhqk,ijkhd->ijqhd", grad_scores, k_tiles)
    grad_k_tiles = product("ijhqk,ijqhd->ijkhd", grad_scores, q_tiles)
    grad_v_tiles = product("ijhqk,ijqhd->ijkhd", softmax_half, g_tiles)
    return (
        query_untile(out_tiles, height, breadth),
        query_untile(grad_q_tiles, height, breadth),
        fold_keys(grad_k_tiles),
        fold_keys(grad_v_tiles),
    )


def return_rims(padded_grads):
    interior = padded_grads[:, :, :, RADIUS:-RADIUS]
    for offset in (1, -1):
        border_part = (
            padded_grads[:, :, :, -RADIUS:] if offset == 1 else padded_grads[:, :, :, :RADIUS]
        )
        arrived = passed_along(border_part, "col", offset)
        if offset == 1:
            interior = interior.at[:, :, :, :RADIUS].add(arrived)
        else:
            interior = interior.at[:, :, :, -RADIUS:].add(arrived)
    owned = interior[:, :, RADIUS:-RADIUS]
    for offset in (1, -1):
        border_part = interior[:, :, -RADIUS:] if offset == 1 else interior[:, :, :RADIUS]
        arrived = passed_along(border_part, "row", offset)
        if offset == 1:
            owned = owned.at[:, :, :RADIUS].add(arrived)
        else:
            owned = owned.at[:, :, -RADIUS:].add(arrived)
    return owned


def body(tokens, w_qkv, w_out, q_saved, k_saved, v_saved, scale_exp, grad_out, crop_start):
    members, height, breadth, features = tokens.shape
    queries = dequantize(q_saved, scale_exp[..., :HEADS])
    keys_full = dequantize(k_saved, scale_exp[..., HEADS : 2 * HEADS])
    values = dequantize(v_saved, scale_exp[..., 2 * HEADS :])
    row_index = lax.axis_index("row")
    col_index = lax.axis_index("col")
    frame_rows = height * lax.axis_size("row")
    frame_cols = breadth * lax.axis_size("col")
    row_place = row_index * height + jnp.arange(height, dtype=jnp.int32)
    col_place = col_index * breadth + jnp.arange(breadth, dtype=jnp.int32)
    inside = (row_place[None, :, None] >= crop_start[:, 0][:, None, None]) & (
        col_place[None, None, :] >= crop_start[:, 1][:, None, None]
    )
    masked = jnp.where(inside[..., None], grad_out, jnp.zeros_like(grad_out))
    flat_grad = masked.reshape(-1, features)
    grad_attn = lax.dot_general(
        flat_grad, w_out, (((1,), (1,)), ((), ())), preferred_element_type=jnp.float32
    )
    grad_attn = grad_attn.astype(jnp.bfloat16).reshape(masked.shape)
    stacked = jnp.stack([keys_full, values])
    padded = padded_2(stacked, (("row", 2), ("col", 3)), RADIUS)

    def one_member(member):
        q_member, g_member, k_member, v_member = member
        return attend(
            q_member,
            g_member,
            k_member,
            v_member,
            row_index * height - RADIUS,
            col_index * breadth - RADIUS,
            frame_rows,
            frame_cols,
        )

    attn_out, grad_query, grad_k_pad, grad_v_pad = lax.map(
        one_member, (queries, grad_attn, padded[0], padded[1])
    )
    owned = return_rims(jnp.stack([grad_k_pad, grad_v_pad]))
    grad_key, grad_value = (owned[0], owned[1])
    flat_qkv = (
        jnp.concatenate([grad_query, grad_key, grad_value], axis=-1)
        .astype(jnp.bfloat16)
        .reshape(-1, 3 * features)
    )
    grad_tokens = lax.dot_general(
        flat_qkv, w_qkv, (((1,), (1,)), ((), ())), preferred_element_type=jnp.float32
    )
    grad_tokens = grad_tokens.astype(jnp.bfloat16).reshape(tokens.shape)
    raw_qkv = lax.dot_general(
        tokens.reshape(-1, features),
        flat_qkv,
        (((0,), (0,)), ((), ())),
        preferred_element_type=jnp.float32,
    )
    raw_out = lax.dot_general(
        attn_out.reshape(-1, features),
        flat_grad,
        (((0,), (0,)), ((), ())),
        preferred_element_type=jnp.float32,
    )
    whole_qkv, whole_out = lax.psum((raw_qkv, raw_out), ("row", "col"))
    squares = jnp.sum(whole_qkv * whole_qkv) + jnp.sum(whole_out * whole_out)
    rows_each = features // lax.axis_size("row")
    qkv_cols = 3 * features // lax.axis_size("col")
    out_cols = features // lax.axis_size("col")
    part_qkv = lax.dynamic_slice(
        whole_qkv, (row_index * rows_each, col_index * qkv_cols), (rows_each, qkv_cols)
    )
    part_out = lax.dynamic_slice(
        whole_out, (row_index * rows_each, col_index * out_cols), (rows_each, out_cols)
    )
    factor = jnp.minimum(1.0, max_norm / jnp.sqrt(squares + tiny_square))
    return (grad_tokens, factor * part_qkv, factor * part_out)


def solution(mesh):
    placed = (
        P(None, "row", "col", None),
        P(),
        P(),
        P(None, "row", "col", None),
        P(None, "row", "col", None),
        P(None, "row", "col", None),
        P(None, "row", "col", None),
        P(None, "row", "col", None),
        P(),
    )
    return jax.shard_map(
        body,
        mesh=mesh,
        in_specs=placed,
        out_specs=(P(None, "row", "col", None), P("row", "col"), P("row", "col")),
        check_vma=False,
    )
```

profile of v0, /device:TPU:0, one launch (start us, length us, event | category | flops | bytes accessed | tf_op | source)
XLA Modules:
  0.0 465.0 jit_solution(9168266061171627752)
XLA Ops:
  10.3 3.8 mul.121
  16.3 3.7 mul.125
  25.1 6.3 %collective-permute-start = (bf16[2,2,4,16,512]{4,3,2,1,0:T(8,128)(2,1)}, bf16[2,2,4,16,512]{4,3,2,1,0:T(8,128)(2,1)}, u32[]{:S(2)}, u32[]{:S(2)}) collective-permute-start(bf16[2,2,4,16,512]{4,3,2,1,0:T(8,128)(2,1)} %get-tuple-element.293), channel_id=1, source_target_pairs={{0,8},{8,16},{16,24},{1,9},{9,17},{17,25},{2,10},{10,18},{18,26},{... | collective-permute-start | bytes 786440 | tf_op jit(solution)/shard_map/ppermute | solution.py:29
  33.6 3.8 mul.131
  48.1 3.2 pad_maximum_fusion.4
  53.1 190.3 %while.24 = (s32[]{:T(128)}, bf16[2,24,16,512]{3,2,1,0:T(8,128)(2,1)}, bf16[2,24,16,512]{3,1,2,0:T(8,128)(2,1)}, f32[2,32,24,512]{3,1,2,0:T(8,128)}, f32[2,32,24...) while((s32[]{:T(128)}, ...), condition=%wide.region_3.4_spmd.clone, body=%wide.region_0.3_spmd.sunk.clone | while | flops 621461056 | bytes 255329296 | solution.py:219
  63.5 4.5 copy.194
  71.7 3.4 copy.196
  77.5 3.3 fusion.117
  81.8 4.4 fusion.120
  93.8 3.5 multiply_convert_fusion.6
  103.0 4.4 convolution_bitcast_fusion.12
  107.4 5.9 %copy.201 = f32[3,2,256,8,64]{4,3,2,1,0:T(8,128)} copy(f32[3,2,256,8,64]{2,4,3,1,0:T(8,128)} %convolution_bitcast_fusion.12) | data formatting | bytes 6291456 | tf_op jit(solution)/shard_map/while/body/eval_jaxpr/ijhqk,ijqhd->ijkhd/transpose | solution.py:39
  113.3 6.2 %reshape.552 = f32[3,2,2,8,2,8,512]{6,5,4,3,2,1,0:T(8,128)} reshape(f32[3,2,256,8,64]{4,3,2,1,0:T(8,128)} %copy.201) | data formatting | bytes 6291456 | tf_op jit(solution)/shard_map/while/body/eval_jaxpr/reshape | solution.py:90
  126.0 5.9 %copy.203 = f32[3,2,256,8,64]{4,3,2,1,0:T(8,128)} copy(f32[3,2,256,8,64]{2,4,3,1,0:T(8,128)} %convolution_bitcast_fusion.13) | data formatting | bytes 6291456 | tf_op jit(solution)/shard_map/while/body/eval_jaxpr/ijhqk,ijqhd->ijkhd/transpose | solution.py:39
  131.8 6.2 %reshape.553 = f32[3,2,2,8,2,8,512]{6,5,4,3,2,1,0:T(8,128)} reshape(f32[3,2,256,8,64]{4,3,2,1,0:T(8,128)} %copy.203) | data formatting | bytes 6291456 | tf_op jit(solution)/shard_map/while/body/eval_jaxpr/reshape | solution.py:90
  158.6 4.5 copy.194
  166.9 3.4 copy.196
  172.7 3.3 fusion.117
  177.0 4.4 fusion.120
  188.9 3.5 multiply_convert_fusion.6
  198.1 4.4 convolution_bitcast_fusion.12
  202.6 5.9 %copy.201 = f32[3,2,256,8,64]{4,3,2,1,0:T(8,128)} copy(f32[3,2,256,8,64]{2,4,3,1,0:T(8,128)} %convolution_bitcast_fusion.12) | data formatting | bytes 6291456 | tf_op jit(solution)/shard_map/while/body/eval_jaxpr/ijhqk,ijqhd->ijkhd/transpose | solution.py:39
  208.5 6.2 %reshape.552 = f32[3,2,2,8,2,8,512]{6,5,4,3,2,1,0:T(8,128)} reshape(f32[3,2,256,8,64]{4,3,2,1,0:T(8,128)} %copy.201) | data formatting | bytes 6291456 | tf_op jit(solution)/shard_map/while/body/eval_jaxpr/reshape | solution.py:90
  221.2 5.9 %copy.203 = f32[3,2,256,8,64]{4,3,2,1,0:T(8,128)} copy(f32[3,2,256,8,64]{2,4,3,1,0:T(8,128)} %convolution_bitcast_fusion.13) | data formatting | bytes 6291456 | tf_op jit(solution)/shard_map/while/body/eval_jaxpr/ijhqk,ijqhd->ijkhd/transpose | solution.py:39
  227.0 6.2 %reshape.553 = f32[3,2,2,8,2,8,512]{6,5,4,3,2,1,0:T(8,128)} reshape(f32[3,2,256,8,64]{4,3,2,1,0:T(8,128)} %copy.203) | data formatting | bytes 6291456 | tf_op jit(solution)/shard_map/while/body/eval_jaxpr/reshape | solution.py:90
  244.9 8.3 %collective-permute-start.4 = (f32[2,2,32,4,512]{4,2,3,1,0:T(8,128)S(1)}, f32[2,2,32,4,512]{4,2,3,1,0:T(8,128)S(1)}, u32[]{:S(2)}, u32[]{:S(2)}) collective-permute-start(f32[2,2,32,4,512]{4,2,3,1,0:T(8,128)S(1)} %fusion.46), channel_id=1, source_target_pairs={{0,1},{1,2},{2,3},{3,4},{4,5},{5,6},{6,7},{8,9},{9,10},{10,11},{11... | collective-permute-start | bytes 3145736 | tf_op jit(solution)/shard_map/ppermute | solution.py:18
  257.2 13.4 %collective-permute-done.5 = f32[2,2,32,4,512]{4,2,3,1,0:T(8,128)S(1)} collective-permute-done((f32[2,2,32,4,512]{4,2,3,1,0:T(8,128)S(1)}, f32[2,2,32,4,512]{4,2,3,1,0:T(8,128)S(1)}, u32[]{:S(2)}, u32[]{:S(2)}) %collective-permute-start.5) | collective-permute-done | bytes 1048608 | tf_op jit(solution)/shard_map/ppermute | solution.py:18
  281.0 4.1 collective-permute-done.7
  285.6 3.2 convolution_bitcast_fusion.3
  293.0 157.2 %all-reduce.11.cloned.1.call-done = (f32[512,1536]{0,1:T(8,128)}, f32[512,512]{1,0:T(8,128)}) async-done(((f32[512,1536]{0,1:T(8,128)}, f32[512,512]{1,0:T(8,128)}), (f32[512,1536]{0,1:T(8,128)}, f32[512,512]{1,0:T(8,128)})) %all-reduce.11.cloned.1.call-update) | async-done | bytes 4194320 | tf_op jit(solution)/shard_map/psum | solution.py:245
  450.2 3.4 multiply_reduce_fusion.1
  (239 shorter events, 142.5 us)
Async XLA Ops:
  7.2 283.5 %copy-start = (bf16[512,1536]{1,0:T(8,128)(2,1)S(1)}, bf16[512,1536]{1,0:T(8,128)(2,1)}, u32[]{:S(2)}) copy-start(bf16[512,1536]{1,0:T(8,128)(2,1)} %param.20) | copy-start | bytes 4718596
  7.2 443.0 %all-reduce.11.cloned.1.call-start = ((), (), s32[]{:S(2)}) async-start(), calls=%async_computation | async-start | bytes 8388608 | tf_op jit(solution)/shard_map/psum | solution.py:245
  23.8 15.5 %collective-permute-start.1 = (bf16[2,2,4,16,512]{4,3,2,1,0:T(8,128)(2,1)}, bf16[2,2,4,16,512]{4,3,2,1,0:T(8,128)(2,1)S(1)}, u32[]{:S(2)}, u32[]{:S(2)}) collective-permute-start(bf16[2,2,4,16,512]{4,3,2,1,0:T(8,128)(2,1)} %get-tuple-element.294), channel_id=1, source_target_pairs={{8,0},{16,8},{24,16},{9,1},{17,9},{25,17},{10,2},{18,10},{26,18},{... | collective-permute-start | bytes 786440 | tf_op jit(solution)/shard_map/ppermute | solution.py:31
  25.1 14.2 %collective-permute-start = (bf16[2,2,4,16,512]{4,3,2,1,0:T(8,128)(2,1)}, bf16[2,2,4,16,512]{4,3,2,1,0:T(8,128)(2,1)}, u32[]{:S(2)}, u32[]{:S(2)}) collective-permute-start(bf16[2,2,4,16,512]{4,3,2,1,0:T(8,128)(2,1)} %get-tuple-element.293), channel_id=1, source_target_pairs={{0,8},{8,16},{16,24},{1,9},{9,17},{17,25},{2,10},{10,18},{18,26},{... | collective-permute-start | bytes 786440 | tf_op jit(solution)/shard_map/ppermute | solution.py:29
  33.6 3.8 copy-start.20
  37.4 7.9 %copy-start.23 = (bf16[512,512]{1,0:T(8,128)(2,1)S(1)}, bf16[512,512]{1,0:T(8,128)(2,1)}, u32[]{:S(2)}) copy-start(bf16[512,512]{1,0:T(8,128)(2,1)} %param.21) | copy-start | bytes 1572868
  37.8 9.1 %copy-start.14 = (f32[2,24,16,512]{3,2,1,0:T(8,128)S(1)}, f32[2,24,16,512]{3,2,1,0:T(8,128)}, u32[]{:S(2)}) copy-start(f32[2,24,16,512]{3,2,1,0:T(8,128)} %mul.131) | copy-start | bytes 4718596
  37.8 9.1 %copy-start.19 = (bf16[2,24,16,512]{3,2,1,0:T(8,128)(2,1)S(1)}, bf16[2,24,16,512]{3,2,1,0:T(8,128)(2,1)}, u32[]{:S(2)}) copy-start(bf16[2,24,16,512]{3,2,1,0:T(8,128)(2,1)} %param.22) | copy-start | bytes 2359300
  39.3 8.8 %copy-start.16 = (bf16[2,24,16,512]{3,2,1,0:T(8,128)(2,1)}, bf16[2,24,16,512]{3,2,1,0:T(8,128)(2,1)S(1)}, u32[]{:S(2)}) copy-start(bf16[2,24,16,512]{3,2,1,0:T(8,128)(2,1)S(1)} %broadcast_select_fusion) | copy-start | bytes 2359300
  41.0 7.1 %collective-permute-start.3 = (bf16[2,2,32,4,512]{4,3,2,1,0:T(4,128)(2,1)S(1)}, bf16[2,2,32,4,512]{4,3,2,1,0:T(4,128)(2,1)S(1)}, u32[]{:S(2)}, u32[]{:S(2)}) collective-permute-start(bf16[2,2,32,4,512]{4,3,2,1,0:T(4,128)(2,1)S(1)} %get-tuple-element.292), channel_id=1, source_target_pairs={{1,0},{2,1},{3,2},{4,3},{5,4},{6,5},{7,6},{9,8},{10,9},{11,10},{12... | collective-permute-start | bytes 1572872 | tf_op jit(solution)/shard_map/ppermute | solution.py:31
  42.3 5.8 %collective-permute-start.2 = (bf16[2,2,32,4,512]{4,3,2,1,0:T(4,128)(2,1)S(1)}, bf16[2,2,32,4,512]{4,3,2,1,0:T(4,128)(2,1)S(1)}, u32[]{:S(2)}, u32[]{:S(2)}) collective-permute-start(bf16[2,2,32,4,512]{4,3,2,1,0:T(4,128)(2,1)S(1)} %get-tuple-element.291), channel_id=1, source_target_pairs={{0,1},{1,2},{2,3},{3,4},{4,5},{5,6},{6,7},{8,9},{9,10},{10,11},{11... | collective-permute-start | bytes 1572872 | tf_op jit(solution)/shard_map/ppermute | solution.py:29
  63.5 4.5 copy-start.7
  81.8 4.4 copy-start.5
  81.8 4.4 copy-start.6
  99.8 3.1 copy-start.4
  140.7 2.8 copy-start.11
  158.6 4.5 copy-start.7
  176.9 4.4 copy-start.5
  176.9 4.4 copy-start.6
  195.0 3.1 copy-start.4
  235.9 2.8 copy-start.11
  243.4 9.8 %copy-start.10 = (f32[2,32,24,512]{3,1,2,0:T(8,128)S(1)}, f32[2,32,24,512]{3,1,2,0:T(8,128)}, u32[]{:S(2)}) copy-start(f32[2,32,24,512]{3,1,2,0:T(8,128)} %get-tuple-element.223) | copy-start | bytes 9437188
  243.5 9.8 %copy-start.13 = (f32[2,32,24,512]{3,1,2,0:T(8,128)S(1)}, f32[2,32,24,512]{3,1,2,0:T(8,128)}, u32[]{:S(2)}) copy-start(f32[2,32,24,512]{3,1,2,0:T(8,128)} %get-tuple-element.224) | copy-start | bytes 9437188
  244.9 10.5 %collective-permute-start.4 = (f32[2,2,32,4,512]{4,2,3,1,0:T(8,128)S(1)}, f32[2,2,32,4,512]{4,2,3,1,0:T(8,128)S(1)}, u32[]{:S(2)}, u32[]{:S(2)}) collective-permute-start(f32[2,2,32,4,512]{4,2,3,1,0:T(8,128)S(1)} %fusion.46), channel_id=1, source_target_pairs={{0,1},{1,2},{2,3},{3,4},{4,5},{5,6},{6,7},{8,9},{9,10},{10,11},{11... | collective-permute-start | bytes 3145736 | tf_op jit(solution)/shard_map/ppermute | solution.py:18
  255.8 19.5 %copy-start.17 = (bf16[2,24,16,512]{3,2,1,0:T(8,128)(2,1)S(1)}, bf16[2,24,16,512]{3,2,1,0:T(8,128)(2,1)}, u32[]{:S(2)}) copy-start(bf16[2,24,16,512]{3,2,1,0:T(8,128)(2,1)} %copy-done.16) | copy-start | bytes 2359300
  255.8 19.5 %copy-start.22 = (bf16[2,24,16,512]{3,2,1,0:T(8,128)(2,1)S(1)}, bf16[2,24,16,512]{3,2,1,0:T(8,128)(2,1)}, u32[]{:S(2)}) copy-start(bf16[2,24,16,512]{3,2,1,0:T(8,128)(2,1)} %get-tuple-element.225) | copy-start | bytes 2359300
  255.8 14.8 %collective-permute-start.5 = (f32[2,2,32,4,512]{4,2,3,1,0:T(8,128)S(1)}, f32[2,2,32,4,512]{4,2,3,1,0:T(8,128)S(1)}, u32[]{:S(2)}, u32[]{:S(2)}) collective-permute-start(f32[2,2,32,4,512]{4,2,3,1,0:T(8,128)S(1)} %get-tuple-element.283), channel_id=1, source_target_pairs={{1,0},{2,1},{3,2},{4,3},{5,4},{6,5},{7,6},{9,8},{10,9},{11,10},{12... | collective-permute-start | bytes 3145736 | tf_op jit(solution)/shard_map/ppermute | solution.py:18
  271.2 9.5 %collective-permute-start.6 = (f32[2,2,4,16,512]{4,2,3,1,0:T(4,128)S(1)}, f32[2,2,4,16,512]{4,2,3,1,0:T(4,128)S(1)}, u32[]{:S(2)}, u32[]{:S(2)}) collective-permute-start(f32[2,2,4,16,512]{4,2,3,1,0:T(4,128)S(1)} %get-tuple-element.286), channel_id=1, source_target_pairs={{0,8},{8,16},{16,24},{1,9},{9,17},{17,25},{2,10},{10,18},{18,26},{... | collective-permute-start | bytes 1572872 | tf_op jit(solution)/shard_map/ppermute | solution.py:18
  274.0 11.1 %collective-permute-start.7 = (f32[2,2,4,16,512]{4,2,3,1,0:T(4,128)S(1)}, f32[2,2,4,16,512]{4,2,3,1,0:T(4,128)S(1)}, u32[]{:S(2)}, u32[]{:S(2)}) collective-permute-start(f32[2,2,4,16,512]{4,2,3,1,0:T(4,128)S(1)} %get-tuple-element.285), channel_id=1, source_target_pairs={{8,0},{16,8},{24,16},{9,1},{17,9},{25,17},{10,2},{18,10},{26,18},{... | collective-permute-start | bytes 1572872 | tf_op jit(solution)/shard_map/ppermute | solution.py:18
  277.6 8.0 %copy-start.18 = (bf16[2,24,16,512]{3,1,2,0:T(8,128)(2,1)S(1)}, bf16[2,24,16,512]{3,1,2,0:T(8,128)(2,1)}, u32[]{:S(2)}) copy-start(bf16[2,24,16,512]{3,1,2,0:T(8,128)(2,1)} %get-tuple-element.222) | copy-start | bytes 2359300
  277.6 8.0 %copy-start.21 = (bf16[2,24,16,512]{3,2,1,0:T(8,128)(2,1)S(1)}, bf16[2,24,16,512]{3,2,1,0:T(8,128)(2,1)}, u32[]{:S(2)}) copy-start(bf16[2,24,16,512]{3,2,1,0:T(8,128)(2,1)} %param.19) | copy-start | bytes 2359300
  450.2 3.4 copy-start.15
  (16 other events, 31.0 us)
Sparse Core Ops, SparseCore 0:
  289.0 161.1 all-reduce.10
where the time goes:
time: 467 us; the launch traced here: 465 us
  waiting for transfers between devices  179 us (38%)
  local copies, waits for them, and re-layouts  162 us (35%)
  matrix products  43.7 us (9%)
  other arithmetic  37.7 us (8%)
  starting transfers between devices  25.9 us (6%)
  between operations  15.8 us (3%)
    psum x1, waiting for transfers between devices, body(): whole_qkv, whole_out = lax.psum((raw_qkv, raw_out), ('row', 'col'))  157 us
    dot_general x12, matrix products, product(): return jnp.einsum(form, left, right, preferred_element_type=jnp.float32)  35 us
    reshape x8, local copies, waits for them, and re-layouts, key_tiles(): paired.transpose(0, 2, 1, 3, 4)  27.9 us
    transpose x6, local copies, waits for them, and re-layouts, product(): return jnp.einsum(form, left, right, preferred_element_type=jnp.float32)  26.7 us
    reshape x4, local copies, waits for them, and re-layouts, fold_keys(): tile_set.reshape(tile_rows, tile_cols, 2, BLOCK, 2, BLOCK, features)  25 us
    ppermute x4, waiting for transfers between devices, passed_along(): return lax.ppermute(array, axis, pairs)  22 us
    while x54, local copies, waits for them, and re-layouts  18.2 us
    mul x9, local copies, waits for them, and re-layouts, dequantize(): mantissa.astype(jnp.float32)  17.7 us
  transfers between devices with their start and end apart: 9, of which 5 were waited for; matrix products, arithmetic and copies ran while one was open for 4% of the time, Pallas kernels for 0%

commit v1 on v0

--- a/solution.py
+++ b/solution.py
@@ -3,6 +3,7 @@
 import jax.numpy as jnp
 from jax import lax
 from jax.sharding import PartitionSpec as P
+from jax.lax import psum
 
 HEADS = 8
 RADIUS = 4
@@ -242,7 +243,7 @@
         (((0,), (0,)), ((), ())),
         preferred_element_type=jnp.float32,
     )
-    whole_qkv, whole_out = lax.psum((raw_qkv, raw_out), ("row", "col"))
+    whole_qkv, whole_out = psum(psum((raw_qkv, raw_out), "col"), "row")
     squares = jnp.sum(whole_qkv * whole_qkv) + jnp.sum(whole_out * whole_out)
     rows_each = features // lax.axis_size("row")
     qkv_cols = 3 * features // lax.axis_size("col")

time: 467 us -> 563 us (1.21)
  waiting for transfers between devices: 179 us -> 275 us
    psum x1 -> x2, waiting for transfers between devices: 157 us -> 253 us  [body(): whole_qkv, whole_out = psum(psum((raw_qkv, raw_out), 'col'), 'row')]
  transfers between devices with their start and end apart: 9 -> 10, of which waited for: 5 -> 6; matrix products, arithmetic and copies ran while one was open for 4% -> 3% of each run, Pallas kernels for 0% -> 0%
where the time goes in v1:
time: 563 us; the launch traced here: 561 us
  waiting for transfers between devices  275 us (49%)
  local copies, waits for them, and re-layouts  162 us (29%)
  matrix products  43.6 us (8%)
  other arithmetic  37.7 us (7%)
  starting transfers between devices  25.9 us (5%)
  between operations  15.8 us (3%)
    psum x2, waiting for transfers between devices, body(): whole_qkv, whole_out = psum(psum((raw_qkv, raw_out), 'col'), 'row')  253 us
    dot_general x12, matrix products, product(): return jnp.einsum(form, left, right, preferred_element_type=jnp.float32)  34.9 us
    reshape x8, local copies, waits for them, and re-layouts, key_tiles(): paired.transpose(0, 2, 1, 3, 4)  28 us
    transpose x6, local copies, waits for them, and re-layouts, product(): return jnp.einsum(form, left, right, preferred_element_type=jnp.float32)  26.7 us
    reshape x4, local copies, waits for them, and re-layouts, fold_keys(): tile_set.reshape(tile_rows, tile_cols, 2, BLOCK, 2, BLOCK, features)  25 us
    ppermute x4, waiting for transfers between devices, passed_along(): return lax.ppermute(array, axis, pairs)  22 us
    while x54, local copies, waits for them, and re-layouts  18.2 us
    mul x9, local copies, waits for them, and re-layouts, dequantize(): mantissa.astype(jnp.float32)  17.7 us
  transfers between devices with their start and end apart: 10, of which 6 were waited for; matrix products, arithmetic and copies ran while one was open for 3% of the time, Pallas kernels for 0%

profile of v1, /device:TPU:0, one launch (start us, length us, event | category | flops | bytes accessed | tf_op | source)
XLA Modules:
  0.0 560.7 jit_solution(5201107886812805060)
XLA Ops:
  10.3 3.8 mul.121
  16.3 3.7 mul.125
  25.1 6.3 %collective-permute-start = (bf16[2,2,4,16,512]{4,3,2,1,0:T(8,128)(2,1)}, bf16[2,2,4,16,512]{4,3,2,1,0:T(8,128)(2,1)}, u32[]{:S(2)}, u32[]{:S(2)}) collective-permute-start(bf16[2,2,4,16,512]{4,3,2,1,0:T(8,128)(2,1)} %get-tuple-element.295), channel_id=1, source_target_pairs={{0,8},{8,16},{16,24},{1,9},{9,17},{17,25},{2,10},{10,18},{18,26},{... | collective-permute-start | bytes 786440 | tf_op jit(solution)/shard_map/ppermute | solution.py:30
  33.6 3.8 mul.131
  53.1 190.3 %while.24 = (s32[]{:T(128)}, bf16[2,24,16,512]{3,2,1,0:T(8,128)(2,1)}, bf16[2,24,16,512]{3,1,2,0:T(8,128)(2,1)}, f32[2,32,24,512]{3,1,2,0:T(8,128)}, f32[2,32,24...) while((s32[]{:T(128)}, ...), condition=%wide.region_3.4_spmd.clone, body=%wide.region_0.3_spmd.sunk.clone | while | flops 621461056 | bytes 255329296 | solution.py:220
  63.5 4.5 copy.194
  71.8 3.4 copy.196
  77.6 3.3 fusion.117
  81.8 4.4 fusion.120
  93.8 3.5 multiply_convert_fusion.6
  103.0 4.4 convolution_bitcast_fusion.12
  107.4 5.9 %copy.201 = f32[3,2,256,8,64]{4,3,2,1,0:T(8,128)} copy(f32[3,2,256,8,64]{2,4,3,1,0:T(8,128)} %convolution_bitcast_fusion.12) | data formatting | bytes 6291456 | tf_op jit(solution)/shard_map/while/body/eval_jaxpr/ijhqk,ijqhd->ijkhd/transpose | solution.py:40
  113.3 6.3 %reshape.552 = f32[3,2,2,8,2,8,512]{6,5,4,3,2,1,0:T(8,128)} reshape(f32[3,2,256,8,64]{4,3,2,1,0:T(8,128)} %copy.201) | data formatting | bytes 6291456 | tf_op jit(solution)/shard_map/while/body/eval_jaxpr/reshape | solution.py:91
  126.0 5.9 %copy.203 = f32[3,2,256,8,64]{4,3,2,1,0:T(8,128)} copy(f32[3,2,256,8,64]{2,4,3,1,0:T(8,128)} %convolution_bitcast_fusion.13) | data formatting | bytes 6291456 | tf_op jit(solution)/shard_map/while/body/eval_jaxpr/ijhqk,ijqhd->ijkhd/transpose | solution.py:40
  131.8 6.3 %reshape.553 = f32[3,2,2,8,2,8,512]{6,5,4,3,2,1,0:T(8,128)} reshape(f32[3,2,256,8,64]{4,3,2,1,0:T(8,128)} %copy.203) | data formatting | bytes 6291456 | tf_op jit(solution)/shard_map/while/body/eval_jaxpr/reshape | solution.py:91
  158.6 4.5 copy.194
  167.0 3.4 copy.196
  172.7 3.3 fusion.117
  177.0 4.4 fusion.120
  188.9 3.5 multiply_convert_fusion.6
  198.2 4.4 convolution_bitcast_fusion.12
  202.6 5.9 %copy.201 = f32[3,2,256,8,64]{4,3,2,1,0:T(8,128)} copy(f32[3,2,256,8,64]{2,4,3,1,0:T(8,128)} %convolution_bitcast_fusion.12) | data formatting | bytes 6291456 | tf_op jit(solution)/shard_map/while/body/eval_jaxpr/ijhqk,ijqhd->ijkhd/transpose | solution.py:40
  208.5 6.3 %reshape.552 = f32[3,2,2,8,2,8,512]{6,5,4,3,2,1,0:T(8,128)} reshape(f32[3,2,256,8,64]{4,3,2,1,0:T(8,128)} %copy.201) | data formatting | bytes 6291456 | tf_op jit(solution)/shard_map/while/body/eval_jaxpr/reshape | solution.py:91
  221.2 5.9 %copy.203 = f32[3,2,256,8,64]{4,3,2,1,0:T(8,128)} copy(f32[3,2,256,8,64]{2,4,3,1,0:T(8,128)} %convolution_bitcast_fusion.13) | data formatting | bytes 6291456 | tf_op jit(solution)/shard_map/while/body/eval_jaxpr/ijhqk,ijqhd->ijkhd/transpose | solution.py:40
  227.0 6.3 %reshape.553 = f32[3,2,2,8,2,8,512]{6,5,4,3,2,1,0:T(8,128)} reshape(f32[3,2,256,8,64]{4,3,2,1,0:T(8,128)} %copy.203) | data formatting | bytes 6291456 | tf_op jit(solution)/shard_map/while/body/eval_jaxpr/reshape | solution.py:91
  244.9 8.3 %collective-permute-start.4 = (f32[2,2,32,4,512]{4,2,3,1,0:T(8,128)S(1)}, f32[2,2,32,4,512]{4,2,3,1,0:T(8,128)S(1)}, u32[]{:S(2)}, u32[]{:S(2)}) collective-permute-start(f32[2,2,32,4,512]{4,2,3,1,0:T(8,128)S(1)} %fusion.46), channel_id=1, source_target_pairs={{0,1},{1,2},{2,3},{3,4},{4,5},{5,6},{6,7},{8,9},{9,10},{10,11},{11... | collective-permute-start | bytes 3145736 | tf_op jit(solution)/shard_map/ppermute | solution.py:19
  257.2 13.4 %collective-permute-done.5 = f32[2,2,32,4,512]{4,2,3,1,0:T(8,128)S(1)} collective-permute-done((f32[2,2,32,4,512]{4,2,3,1,0:T(8,128)S(1)}, f32[2,2,32,4,512]{4,2,3,1,0:T(8,128)S(1)}, u32[]{:S(2)}, u32[]{:S(2)}) %collective-permute-start.5) | collective-permute-done | bytes 1048608 | tf_op jit(solution)/shard_map/ppermute | solution.py:19
  280.9 4.1 collective-permute-done.7
  285.6 3.2 convolution_bitcast_fusion.3
  288.9 99.5 %all-reduce.13.cloned.1.call-done = (f32[512,1536]{0,1:T(8,128)}, f32[512,512]{1,0:T(8,128)}) async-done(((f32[512,1536]{0,1:T(8,128)}, f32[512,512]{1,0:T(8,128)}), (f32[512,1536]{0,1:T(8,128)}, f32[512,512]{1,0:T(8,128)})) %all-reduce.13.cloned.1.call-update) | async-done | bytes 4194320 | tf_op jit(solution)/shard_map/psum | solution.py:246
  392.6 153.3 %all-reduce.15.cloned.1.call-done = (f32[512,1536]{0,1:T(8,128)}, f32[512,512]{1,0:T(8,128)}) async-done(((f32[512,1536]{0,1:T(8,128)}, f32[512,512]{1,0:T(8,128)}), (f32[512,1536]{0,1:T(8,128)}, f32[512,512]{1,0:T(8,128)})) %all-reduce.15.cloned.1.call-update) | async-done | bytes 4194320 | tf_op jit(solution)/shard_map/psum | solution.py:246
  545.9 3.4 multiply_reduce_fusion.1
  (242 shorter events, 145.8 us)
Async XLA Ops:
  7.2 383.1 %copy-start = (bf16[512,1536]{1,0:T(8,128)(2,1)S(1)}, bf16[512,1536]{1,0:T(8,128)(2,1)}, u32[]{:S(2)}) copy-start(bf16[512,1536]{1,0:T(8,128)(2,1)} %param.20) | copy-start | bytes 4718596
  7.2 381.2 %all-reduce.13.cloned.1.call-start = ((), (), s32[]{:S(2)}) async-start(), calls=%async_computation | async-start | bytes 8388608 | tf_op jit(solution)/shard_map/psum | solution.py:246
  23.8 15.5 %collective-permute-start.1 = (bf16[2,2,4,16,512]{4,3,2,1,0:T(8,128)(2,1)}, bf16[2,2,4,16,512]{4,3,2,1,0:T(8,128)(2,1)S(1)}, u32[]{:S(2)}, u32[]{:S(2)}) collective-permute-start(bf16[2,2,4,16,512]{4,3,2,1,0:T(8,128)(2,1)} %get-tuple-element.296), channel_id=1, source_target_pairs={{8,0},{16,8},{24,16},{9,1},{17,9},{25,17},{10,2},{18,10},{26,18},{... | collective-permute-start | bytes 786440 | tf_op jit(solution)/shard_map/ppermute | solution.py:32
  25.1 14.2 %collective-permute-start = (bf16[2,2,4,16,512]{4,3,2,1,0:T(8,128)(2,1)}, bf16[2,2,4,16,512]{4,3,2,1,0:T(8,128)(2,1)}, u32[]{:S(2)}, u32[]{:S(2)}) collective-permute-start(bf16[2,2,4,16,512]{4,3,2,1,0:T(8,128)(2,1)} %get-tuple-element.295), channel_id=1, source_target_pairs={{0,8},{8,16},{16,24},{1,9},{9,17},{17,25},{2,10},{10,18},{18,26},{... | collective-permute-start | bytes 786440 | tf_op jit(solution)/shard_map/ppermute | solution.py:30
  33.6 3.8 copy-start.20
  37.4 7.9 %copy-start.23 = (bf16[512,512]{1,0:T(8,128)(2,1)S(1)}, bf16[512,512]{1,0:T(8,128)(2,1)}, u32[]{:S(2)}) copy-start(bf16[512,512]{1,0:T(8,128)(2,1)} %param.21) | copy-start | bytes 1572868
  37.8 9.1 %copy-start.14 = (f32[2,24,16,512]{3,2,1,0:T(8,128)S(1)}, f32[2,24,16,512]{3,2,1,0:T(8,128)}, u32[]{:S(2)}) copy-start(f32[2,24,16,512]{3,2,1,0:T(8,128)} %mul.131) | copy-start | bytes 4718596
  37.8 9.1 %copy-start.19 = (bf16[2,24,16,512]{3,2,1,0:T(8,128)(2,1)S(1)}, bf16[2,24,16,512]{3,2,1,0:T(8,128)(2,1)}, u32[]{:S(2)}) copy-start(bf16[2,24,16,512]{3,2,1,0:T(8,128)(2,1)} %param.22) | copy-start | bytes 2359300
  39.3 8.8 %copy-start.16 = (bf16[2,24,16,512]{3,2,1,0:T(8,128)(2,1)}, bf16[2,24,16,512]{3,2,1,0:T(8,128)(2,1)S(1)}, u32[]{:S(2)}) copy-start(bf16[2,24,16,512]{3,2,1,0:T(8,128)(2,1)S(1)} %broadcast_select_fusion) | copy-start | bytes 2359300
  40.9 7.1 %collective-permute-start.3 = (bf16[2,2,32,4,512]{4,3,2,1,0:T(4,128)(2,1)S(1)}, bf16[2,2,32,4,512]{4,3,2,1,0:T(4,128)(2,1)S(1)}, u32[]{:S(2)}, u32[]{:S(2)}) collective-permute-start(bf16[2,2,32,4,512]{4,3,2,1,0:T(4,128)(2,1)S(1)} %get-tuple-element.294), channel_id=1, source_target_pairs={{1,0},{2,1},{3,2},{4,3},{5,4},{6,5},{7,6},{9,8},{10,9},{11,10},{12... | collective-permute-start | bytes 1572872 | tf_op jit(solution)/shard_map/ppermute | solution.py:32
  42.2 5.8 %collective-permute-start.2 = (bf16[2,2,32,4,512]{4,3,2,1,0:T(4,128)(2,1)S(1)}, bf16[2,2,32,4,512]{4,3,2,1,0:T(4,128)(2,1)S(1)}, u32[]{:S(2)}, u32[]{:S(2)}) collective-permute-start(bf16[2,2,32,4,512]{4,3,2,1,0:T(4,128)(2,1)S(1)} %get-tuple-element.293), channel_id=1, source_target_pairs={{0,1},{1,2},{2,3},{3,4},{4,5},{5,6},{6,7},{8,9},{9,10},{10,11},{11... | collective-permute-start | bytes 1572872 | tf_op jit(solution)/shard_map/ppermute | solution.py:30
  63.5 4.5 copy-start.7
  81.8 4.4 copy-start.5
  81.8 4.4 copy-start.6
  99.9 3.1 copy-start.4
  140.7 2.8 copy-start.11
  158.6 4.5 copy-start.7
  177.0 4.4 copy-start.5
  177.0 4.4 copy-start.6
  195.0 3.1 copy-start.4
  243.4 9.8 %copy-start.10 = (f32[2,32,24,512]{3,1,2,0:T(8,128)S(1)}, f32[2,32,24,512]{3,1,2,0:T(8,128)}, u32[]{:S(2)}) copy-start(f32[2,32,24,512]{3,1,2,0:T(8,128)} %get-tuple-element.223) | copy-start | bytes 9437188
  243.4 9.8 %copy-start.13 = (f32[2,32,24,512]{3,1,2,0:T(8,128)S(1)}, f32[2,32,24,512]{3,1,2,0:T(8,128)}, u32[]{:S(2)}) copy-start(f32[2,32,24,512]{3,1,2,0:T(8,128)} %get-tuple-element.224) | copy-start | bytes 9437188
  244.9 10.5 %collective-permute-start.4 = (f32[2,2,32,4,512]{4,2,3,1,0:T(8,128)S(1)}, f32[2,2,32,4,512]{4,2,3,1,0:T(8,128)S(1)}, u32[]{:S(2)}, u32[]{:S(2)}) collective-permute-start(f32[2,2,32,4,512]{4,2,3,1,0:T(8,128)S(1)} %fusion.46), channel_id=1, source_target_pairs={{0,1},{1,2},{2,3},{3,4},{4,5},{5,6},{6,7},{8,9},{9,10},{10,11},{11... | collective-permute-start | bytes 3145736 | tf_op jit(solution)/shard_map/ppermute | solution.py:19
  255.8 19.5 %copy-start.17 = (bf16[2,24,16,512]{3,2,1,0:T(8,128)(2,1)S(1)}, bf16[2,24,16,512]{3,2,1,0:T(8,128)(2,1)}, u32[]{:S(2)}) copy-start(bf16[2,24,16,512]{3,2,1,0:T(8,128)(2,1)} %copy-done.16) | copy-start | bytes 2359300
  255.8 19.5 %copy-start.22 = (bf16[2,24,16,512]{3,2,1,0:T(8,128)(2,1)S(1)}, bf16[2,24,16,512]{3,2,1,0:T(8,128)(2,1)}, u32[]{:S(2)}) copy-start(bf16[2,24,16,512]{3,2,1,0:T(8,128)(2,1)} %get-tuple-element.225) | copy-start | bytes 2359300
  255.8 14.8 %collective-permute-start.5 = (f32[2,2,32,4,512]{4,2,3,1,0:T(8,128)S(1)}, f32[2,2,32,4,512]{4,2,3,1,0:T(8,128)S(1)}, u32[]{:S(2)}, u32[]{:S(2)}) collective-permute-start(f32[2,2,32,4,512]{4,2,3,1,0:T(8,128)S(1)} %get-tuple-element.285), channel_id=1, source_target_pairs={{1,0},{2,1},{3,2},{4,3},{5,4},{6,5},{7,6},{9,8},{10,9},{11,10},{12... | collective-permute-start | bytes 3145736 | tf_op jit(solution)/shard_map/ppermute | solution.py:19
  271.1 9.5 %collective-permute-start.6 = (f32[2,2,4,16,512]{4,2,3,1,0:T(4,128)S(1)}, f32[2,2,4,16,512]{4,2,3,1,0:T(4,128)S(1)}, u32[]{:S(2)}, u32[]{:S(2)}) collective-permute-start(f32[2,2,4,16,512]{4,2,3,1,0:T(4,128)S(1)} %get-tuple-element.288), channel_id=1, source_target_pairs={{0,8},{8,16},{16,24},{1,9},{9,17},{17,25},{2,10},{10,18},{18,26},{... | collective-permute-start | bytes 1572872 | tf_op jit(solution)/shard_map/ppermute | solution.py:19
  274.0 11.1 %collective-permute-start.7 = (f32[2,2,4,16,512]{4,2,3,1,0:T(4,128)S(1)}, f32[2,2,4,16,512]{4,2,3,1,0:T(4,128)S(1)}, u32[]{:S(2)}, u32[]{:S(2)}) collective-permute-start(f32[2,2,4,16,512]{4,2,3,1,0:T(4,128)S(1)} %get-tuple-element.287), channel_id=1, source_target_pairs={{8,0},{16,8},{24,16},{9,1},{17,9},{25,17},{10,2},{18,10},{26,18},{... | collective-permute-start | bytes 1572872 | tf_op jit(solution)/shard_map/ppermute | solution.py:19
  277.5 8.0 %copy-start.18 = (bf16[2,24,16,512]{3,1,2,0:T(8,128)(2,1)S(1)}, bf16[2,24,16,512]{3,1,2,0:T(8,128)(2,1)}, u32[]{:S(2)}) copy-start(bf16[2,24,16,512]{3,1,2,0:T(8,128)(2,1)} %get-tuple-element.222) | copy-start | bytes 2359300
  277.5 8.0 %copy-start.21 = (bf16[2,24,16,512]{3,2,1,0:T(8,128)(2,1)S(1)}, bf16[2,24,16,512]{3,2,1,0:T(8,128)(2,1)}, u32[]{:S(2)}) copy-start(bf16[2,24,16,512]{3,2,1,0:T(8,128)(2,1)} %param.19) | copy-start | bytes 2359300
  288.8 257.0 %all-reduce.15.cloned.1.call-start = ((), (), s32[]{:S(2)}) async-start(), calls=%async_computation.1 | async-start | bytes 8388608 | tf_op jit(solution)/shard_map/psum | solution.py:246
  545.9 3.4 copy-start.15
  (17 other events, 33.8 us)
Sparse Core Ops, SparseCore 0:
  289.0 99.3 all-reduce.12
  390.8 155.0 all-reduce.14
